TPU v7x, 32 devices: a whole 2x2x4 slice. The times are simulated.
32 devices in a mesh: dp: 8 (over z, x), tensor: 4 (over y, core).
Axes of the slice: x: 2, y: 2, z: 4, core: 2. Of those that a mesh axis runs over, the one named last changes fastest.
Arguments:
- tokens_in: bfloat16 [16384, 1152], P(('dp', 'tensor')), may hold values from -6 to 6
- condition: bfloat16 [16, 1152], P('dp'), may hold values from -6 to 6
- w_ada: bfloat16 [1152, 6912], P('dp', 'tensor'), may hold values from -0.1875 to 0.1875
- b_ada: bfloat16 [6912], P('tensor'), may hold values from -3 to 3
- w_qkv: bfloat16 [1152, 3456], P('dp', 'tensor'), may hold values from -0.1875 to 0.1875
- b_qv: bfloat16 [2304], P('tensor'), may hold values from -3 to 3
- w_proj: bfloat16 [1152, 1152], P('tensor', 'dp'), may hold values from -2 to 2
- b_proj: bfloat16 [1152], replicated, may hold values from -3 to 3
- w_fc1: bfloat16 [1152, 4608], P('dp', 'tensor'), may hold values from -0.1875 to 0.1875
- b_fc1: bfloat16 [4608], P('tensor'), may hold values from -3 to 3
- w_fc2: bfloat16 [4608, 1152], P('tensor', 'dp'), may hold values from -0.09375 to 0.09375
- b_fc2: bfloat16 [1152], replicated, may hold values from -3 to 3
- cotangent: bfloat16 [16384, 1152], P(('dp', 'tensor')), may hold values from -6 to 6
Outputs:
- block_out: bfloat16 [16384, 1152], P(('dp', 'tensor'))
- grad_tokens: float32 [16384, 1152], P(('dp', 'tensor'))
- grad_condition: float32 [16, 1152], P('dp')
- grad_w_ada: float32 [1152, 6912], P('dp', 'tensor')
- grad_b_ada: float32 [6912], P('tensor')
- grad_w_qkv: float32 [1152, 3456], P('dp', 'tensor')
- grad_b_qv: float32 [2304], P('tensor')
- grad_w_proj: float32 [1152, 1152], P('tensor', 'dp')
- grad_b_proj: float32 [1152], replicated
- grad_w_fc1: float32 [1152, 4608], P('dp', 'tensor')
- grad_b_fc1: float32 [4608], P('tensor')
- grad_w_fc2: float32 [4608, 1152], P('tensor', 'dp')
- grad_b_fc2: float32 [1152], replicated
All inputs are finite; a program needn't handle non-finite values.
Results may differ from a plain program's by a relative error of at most 0.015.
The roundings to bfloat16 on the way count: a program that leaves them out, or rounds other values in their place, can miss the bound.
Values may be sent and summed in bfloat16 or wider, within the bound.
No kernel may reach another device: no remote copies, remote signals or barrier semaphores. Data moves between devices by JAX's collectives and lax.ppermute only.
A program may use at most 192 MiB of HBM per device.

v0:
```python
import jax
import jax.numpy as jnp
from jax import lax
from jax.sharding import PartitionSpec as P

HEAD_DIM = 72
SEQ = 1024
highest = lax.Precision.HIGHEST
root_two_pi = 0.7978845608028654
cubic_term = 0.044715
epsilon = 1e-06


def normalize(values):
    centre = values - jnp.mean(values, axis=-1, keepdims=True)
    inverse = lax.rsqrt(jnp.mean(centre * centre, axis=-1, keepdims=True) + epsilon)
    return (centre * inverse, inverse)


def norm_back(normed, inverse, grad_in):
    mean_grad = jnp.mean(grad_in, axis=-1, keepdims=True)
    mean_cross = jnp.mean(grad_in * normed, axis=-1, keepdims=True)
    return inverse * (grad_in - mean_grad - normed * mean_cross)


def gelu_parts(pre_act):
    tangent = jnp.tanh(root_two_pi * (pre_act + cubic_term * pre_act * pre_act * pre_act))
    activated = 0.5 * pre_act * (1.0 + tangent)
    gelu_slope = 0.5 * (1.0 + tangent) + 0.5 * pre_act * (1.0 - tangent * tangent) * root_two_pi * (
        1.0 + 3.0 * cubic_term * pre_act * pre_act
    )
    return (activated, gelu_slope)


def fetch_weights(w_qkv, w_fc1, w_ada, w_proj, w_fc2):
    columns = (
        lax.all_gather(w_qkv, "dp", axis=0, tiled=True),
        lax.all_gather(w_fc1, "dp", axis=0, tiled=True),
        lax.all_gather(w_ada, "dp", axis=0, tiled=True),
    )
    row_parts = (
        lax.all_gather(w_proj, "dp", axis=1, tiled=True),
        lax.all_gather(w_fc2, "dp", axis=1, tiled=True),
    )
    return (columns, row_parts)


def gather_rows(values):
    return lax.all_gather(values, "tensor", axis=0, tiled=True)


def sum_back(row_term, row_count):
    return lax.psum_scatter(
        row_term(jnp.int32(0), lax.axis_size("tensor") * row_count).astype(jnp.bfloat16),
        "tensor",
        scatter_dimension=0,
        tiled=True,
    ).astype(jnp.float32)


def right_product(left_rows, right_mat):
    return jnp.dot(left_rows, right_mat, preferred_element_type=jnp.float32)


def transposed_product(left_rows, right_mat):

    def row_term(row_start, row_count):
        return lax.dot_general(
            left_rows, right_mat, (((1,), (1,)), ((), ())), preferred_element_type=jnp.float32
        )

    return row_term


def back_fold(weight_mat, kept_all, shard_rows):
    rows_in = lax.dot_general(
        shard_rows, weight_mat, (((1,), (1,)), ((), ())), preferred_element_type=jnp.float32
    )
    grad_weight = lax.dot_general(
        kept_all, shard_rows, (((0,), (0,)), ((), ())), preferred_element_type=jnp.float32
    )
    return (rows_in, grad_weight)


def attend(operands):
    queries, keys_b, values_b = operands
    score_scale = queries.shape[-1] ** (-0.5)
    scores = (
        jnp.einsum("qhd,khd->hqk", queries, keys_b, preferred_element_type=jnp.float32)
        * score_scale
    )
    row_max = jnp.max(scores, axis=-1, keepdims=True)
    exponent = jnp.exp(scores - row_max)
    row_total = jnp.sum(exponent, axis=-1, keepdims=True)
    attn_probs = (exponent / row_total).astype(jnp.bfloat16)
    mixture = jnp.einsum("hqk,khd->qhd", attn_probs, values_b, preferred_element_type=jnp.float32)
    return (mixture.astype(jnp.bfloat16), (row_max + jnp.log(row_total))[..., 0])


def attend_back(operands):
    queries, keys_b, values_b, grad_mix, logsum = operands
    score_scale = queries.shape[-1] ** (-0.5)
    scores = (
        jnp.einsum("qhd,khd->hqk", queries, keys_b, preferred_element_type=jnp.float32)
        * score_scale
    )
    attn_probs = jnp.exp(scores - logsum[..., None])
    grad_probs = jnp.einsum("qhd,khd->hqk", grad_mix, values_b, preferred_element_type=jnp.float32)
    row_inner = jnp.sum(grad_probs * attn_probs, axis=-1, keepdims=True)
    grad_scores = (attn_probs * (grad_probs - row_inner)).astype(jnp.bfloat16)
    grad_queries = (
        jnp.einsum("hqk,khd->qhd", grad_scores, keys_b, preferred_element_type=jnp.float32)
        * score_scale
    )
    grad_keys = (
        jnp.einsum("hqk,qhd->khd", grad_scores, queries, preferred_element_type=jnp.float32)
        * score_scale
    )
    grad_values = jnp.einsum(
        "hqk,qhd->khd",
        attn_probs.astype(jnp.bfloat16),
        grad_mix,
        preferred_element_type=jnp.float32,
    )
    return jnp.stack([grad_queries, grad_keys, grad_values], axis=2).astype(jnp.bfloat16)


def shards(
    tokens_in,
    condition,
    w_ada,
    b_ada,
    w_qkv,
    b_qv,
    w_proj,
    b_proj,
    w_fc1,
    b_fc1,
    w_fc2,
    b_fc2,
    cotangent,
):
    tok_rows = tokens_in.shape[0]
    latents = condition.shape[0]
    head_size = HEAD_DIM
    (qkv_full, fc1_full, ada_full), (proj_full, fc2_full) = fetch_weights(
        w_qkv, w_fc1, w_ada, w_proj, w_fc2
    )
    cond_vals = condition.astype(jnp.float32)
    cond_sigmoid = jax.nn.sigmoid(cond_vals)
    silu_cond = (cond_vals * cond_sigmoid).astype(jnp.bfloat16)
    mod_part = jnp.dot(silu_cond, ada_full, preferred_element_type=jnp.float32) + b_ada.astype(
        jnp.float32
    )
    modulation = lax.all_gather(mod_part, "tensor", axis=1, tiled=True)
    row_place = lax.axis_index("tensor") * tok_rows + jnp.arange(tok_rows, dtype=jnp.int32)
    onehot = (row_place[:, None] // SEQ == jnp.arange(latents, dtype=jnp.int32)[None, :]).astype(
        jnp.float32
    )
    mod_rows = jnp.dot(onehot, modulation, precision=highest)
    shift_attn, scale_attn, gate_attn, shift_mlp, scale_mlp, gate_mlp = jnp.split(
        mod_rows, 6, axis=1
    )
    input_vals = tokens_in.astype(jnp.float32)
    normed_one, inverse_one = normalize(input_vals)
    attn_in = (normed_one * (1.0 + scale_attn) + shift_attn).astype(jnp.bfloat16)
    attn_rows = gather_rows(attn_in)
    full_rows = attn_rows.shape[0]
    head_count = qkv_full.shape[1] // (3 * head_size)
    projected = jnp.dot(attn_rows, qkv_full, preferred_element_type=jnp.float32).reshape(
        full_rows, head_count, 3, head_size
    )
    bias_qv = b_qv.astype(jnp.float32).reshape(head_count, 2, head_size)
    block_shape = (full_rows // SEQ, SEQ, head_count, head_size)
    queries = (projected[:, :, 0] + bias_qv[:, 0]).astype(jnp.bfloat16).reshape(block_shape)
    keys_b = projected[:, :, 1].astype(jnp.bfloat16).reshape(block_shape)
    values_b = (projected[:, :, 2] + bias_qv[:, 1]).astype(jnp.bfloat16).reshape(block_shape)
    mixture, logsum = lax.map(attend, (queries, keys_b, values_b))
    mix_rows = mixture.reshape(full_rows, head_count * head_size)
    attn_out = lax.psum_scatter(
        right_product(mix_rows, proj_full).astype(jnp.bfloat16),
        "tensor",
        scatter_dimension=0,
        tiled=True,
    ).astype(jnp.float32) + b_proj.astype(jnp.float32)
    middle = input_vals + gate_attn * attn_out
    normed_two, inverse_two = normalize(middle)
    mlp_in = (normed_two * (1.0 + scale_mlp) + shift_mlp).astype(jnp.bfloat16)
    mlp_rows = gather_rows(mlp_in)
    pre_act = jnp.dot(mlp_rows, fc1_full, preferred_element_type=jnp.float32) + b_fc1.astype(
        jnp.float32
    )
    activated, gelu_slope = gelu_parts(pre_act)
    act_rows = activated.astype(jnp.bfloat16)
    mlp_out = lax.psum_scatter(
        right_product(act_rows, fc2_full).astype(jnp.bfloat16),
        "tensor",
        scatter_dimension=0,
        tiled=True,
    ).astype(jnp.float32) + b_fc2.astype(jnp.float32)
    result = middle + gate_mlp * mlp_out
    grad_out = cotangent.astype(jnp.float32)
    grad_mlp = (gate_mlp * grad_out).astype(jnp.bfloat16)
    d_gate_mlp = grad_out * mlp_out
    held_weights = lax.optimization_barrier((w_qkv, w_fc1, w_ada, w_proj, w_fc2, grad_mlp))
    (qkv_back, fc1_back, ada_back), (proj_back, fc2_back) = fetch_weights(
        held_weights[0], held_weights[1], held_weights[2], held_weights[3], held_weights[4]
    )
    grad_act, grad_fc2 = back_fold(
        fc2_back, act_rows, lax.all_gather(grad_mlp, "tensor", axis=0, tiled=True)
    )
    grad_pre = (grad_act * gelu_slope).astype(jnp.bfloat16)
    grad_fc1 = lax.dot_general(
        mlp_rows, grad_pre, (((0,), (0,)), ((), ())), preferred_element_type=jnp.float32
    )
    grad_mlp_in = sum_back(transposed_product(grad_pre, fc1_back), tok_rows)
    d_scale_mlp = grad_mlp_in * normed_two
    grad_middle = grad_out + norm_back(normed_two, inverse_two, grad_mlp_in * (1.0 + scale_mlp))
    grad_attn = (gate_attn * grad_middle).astype(jnp.bfloat16)
    d_gate_attn = grad_middle * attn_out
    grad_mixture, grad_proj = back_fold(
        proj_back, mix_rows, lax.all_gather(grad_attn, "tensor", axis=0, tiled=True)
    )
    grad_mix_b = grad_mixture.astype(jnp.bfloat16).reshape(block_shape)
    grad_qkv = lax.map(attend_back, (queries, keys_b, values_b, grad_mix_b, logsum)).reshape(
        full_rows, head_count * 3 * head_size
    )
    grad_wqkv = lax.dot_general(
        attn_rows, grad_qkv, (((0,), (0,)), ((), ())), preferred_element_type=jnp.float32
    )
    grad_attn_in = sum_back(transposed_product(grad_qkv, qkv_back), tok_rows)
    d_scale_attn = grad_attn_in * normed_one
    grad_tokens = grad_middle + norm_back(
        normed_one, inverse_one, grad_attn_in * (1.0 + scale_attn)
    )
    grad_mod_rows = jnp.concatenate(
        [grad_attn_in, d_scale_attn, d_gate_attn, grad_mlp_in, d_scale_mlp, d_gate_mlp], axis=1
    )
    grad_mod_all = jnp.dot(onehot.T, grad_mod_rows, precision=highest)
    grad_mod = lax.psum_scatter(
        grad_mod_all.astype(jnp.bfloat16), "tensor", scatter_dimension=1, tiled=True
    ).astype(jnp.float32)
    grad_ada = jnp.dot(silu_cond.astype(jnp.float32).T, grad_mod, precision=highest)
    grad_silu = jnp.dot(grad_mod, ada_back.T, precision=highest)
    grad_cond_part = grad_silu * cond_sigmoid * (1.0 + cond_vals * (1.0 - cond_sigmoid))
    qkv_sums = jnp.sum(
        grad_qkv.astype(jnp.float32).reshape(full_rows, head_count, 3, head_size), axis=0
    )
    grad_bqv_part = jnp.stack([qkv_sums[:, 0], qkv_sums[:, 2]], axis=1).reshape(-1)
    grad_b1_part = jnp.sum(grad_pre.astype(jnp.float32), axis=0)
    grad_bo_part = jnp.sum(grad_attn.astype(jnp.float32), axis=0)
    grad_b2_part = jnp.sum(grad_mlp.astype(jnp.float32), axis=0)
    grad_ba_part = jnp.sum(grad_mod, axis=0)
    grad_condition, grad_bo_mid, grad_b2_mid = lax.psum(
        (grad_cond_part, grad_bo_part, grad_b2_part), "tensor"
    )
    grad_bqv, grad_b1, grad_ba, grad_bo, grad_b2 = lax.psum(
        (grad_bqv_part, grad_b1_part, grad_ba_part, grad_bo_mid, grad_b2_mid), "dp"
    )
    owned_qkv, owned_fc1, owned_ada = (
        lax.psum_scatter(grad_wqkv, "dp", scatter_dimension=0, tiled=True),
        lax.psum_scatter(grad_fc1, "dp", scatter_dimension=0, tiled=True),
        lax.psum_scatter(grad_ada, "dp", scatter_dimension=0, tiled=True),
    )
    owned_proj, owned_fc2 = (
        lax.psum_scatter(grad_proj, "dp", scatter_dimension=1, tiled=True),
        lax.psum_scatter(grad_fc2, "dp", scatter_dimension=1, tiled=True),
    )
    return (
        result.astype(jnp.bfloat16),
        grad_tokens,
        grad_condition,
        owned_ada,
        grad_ba,
        owned_qkv,
        grad_bqv,
        owned_proj,
        grad_bo,
        owned_fc1,
        grad_b1,
        owned_fc2,
        grad_b2,
    )


def solution(mesh):
    placed = (
        P(("dp", "tensor"), None),
        P("dp", None),
        P("dp", "tensor"),
        P("tensor"),
        P("dp", "tensor"),
        P("tensor"),
        P("tensor", "dp"),
        P(),
        P("dp", "tensor"),
        P("tensor"),
        P("tensor", "dp"),
        P(),
        P(("dp", "tensor"), None),
    )
    return jax.shard_map(
        shards,
        mesh=mesh,
        in_specs=placed,
        out_specs=(
            P(("dp", "tensor"), None),
            P(("dp", "tensor"), None),
            P("dp", None),
            P("dp", "tensor"),
            P("tensor"),
            P("dp", "tensor"),
            P("tensor"),
            P("tensor", "dp"),
            P(),
            P("dp", "tensor"),
            P("tensor"),
            P("tensor", "dp"),
            P(),
        ),
        check_vma=False,
    )
```

profile of v0, /device:TPU:0, one launch (start us, length us, event | category | flops | bytes accessed | tf_op | source)
XLA Modules:
  0.0 1585.1 jit_solution(13999615193881543100)
XLA Ops:
  11.4 74.1 %all-gather.14.cloned.1.call-done = bf16[1152,1728]{1,0:T(8,128)(2,1)} async-done(((bf16[144,1728]{1,0:T(8,128)(2,1)}), bf16[1152,1728]{1,0:T(8,128)(2,1)}) %all-gather.14.cloned.1.call-update) | async-done | bytes 3981328 | tf_op jit(solution)/shard_map/all_gather | solution.py:39
  88.3 5.2 all-gather
  93.7 5.7 fusion.77
  99.5 5.0 copy-done.1
  106.3 36.6 %all_gather.49 = bf16[288,1152]{0,1:T(8,128)(2,1)} all-gather(bf16[288,144]{0,1:T(8,128)(2,1)S(1)} %copy-done.24), channel_id=1, replica_groups=mesh['dp'=8,'tensor'=4] {'dp'}, dimensions={1}, use_global_device_ids=true | all-gather | bytes 746496 | tf_op jit(solution)/shard_map/all_gather | solution.py:42
  142.9 4.1 all-gather.18.cloned.1.call-done
  147.1 39.3 %all-gather.16.cloned.1.call-done = bf16[2048,1152]{1,0:T(8,128)(2,1)} async-done(((bf16[512,1152]{1,0:T(8,128)(2,1)}), bf16[2048,1152]{1,0:T(8,128)(2,1)}) %all-gather.16.cloned.1.call-update) | async-done | bytes 4718608 | tf_op jit(solution)/shard_map/all_gather | solution.py:49
  186.4 7.4 fusion.101
  201.0 4.2 squeeze.32
  210.3 4.0 convert_element_type.138
  215.9 51.3 %while.22 = (s32[]{:T(128)}, bf16[2,1024,4,72]{1,3,2,0:T(8,128)(2,1)}, f32[2,4,1024]{2,1,0:T(4,128)S(1)}, bf16[2,1024,4,72]{1,3,2,0:T(8,128)(2,1)}, bf16[2,1024,...) while((s32[]{:T(128)}, bf16[2,1024,4,72]{1,3,2,0:T(8,128)(2,1)}, ...), condition=%wide.region_5.6_spmd, body=%wide.region_2.5_spmd.sunk | while | flops 1245999104 | bytes 66980012 | solution.py:178
  216.1 8.1 multiply_reduce_fusion.6
  224.2 8.7 fusion.149
  233.0 7.7 fusion.150
  241.7 8.1 multiply_reduce_fusion.6
  249.8 8.7 fusion.149
  258.5 7.7 fusion.150
  271.2 4.5 convolution_convert_fusion.4
  276.6 47.1 %reduce-scatter.13.cloned.1.call-done = bf16[512,1152]{1,0:T(8,128)(2,1)} async-done(((bf16[2048,1152]{1,0:T(8,128)(2,1)}), bf16[512,1152]{1,0:T(8,128)(2,1)}) %reduce-scatter.13.cloned.1.call-update) | async-done | bytes 1179664 | tf_op jit(solution)/shard_map/reduce_scatter | solution.py:180
  328.7 5.6 convert_reduce_fusion.3
  337.3 43.7 %all-gather.22.cloned.1.call-done = bf16[1152,1152]{1,0:T(8,128)(2,1)} async-done(((bf16[144,1152]{1,0:T(8,128)(2,1)}), bf16[1152,1152]{1,0:T(8,128)(2,1)}) %all-gather.22.cloned.1.call-update) | async-done | bytes 2654224 | tf_op jit(solution)/shard_map/all_gather | solution.py:38
  381.0 38.1 %all-gather.20.cloned.1.call-done = bf16[2048,1152]{1,0:T(8,128)(2,1)} async-done(((bf16[512,1152]{1,0:T(8,128)(2,1)}), bf16[2048,1152]{1,0:T(8,128)(2,1)}) %all-gather.20.cloned.1.call-update) | async-done | bytes 4718608 | tf_op jit(solution)/shard_map/all_gather | solution.py:49
  419.2 11.6 convolution_add_fusion
  430.7 45.9 %all-gather.28.cloned.1.call-done = bf16[1152,1152]{0,1:T(8,128)(2,1)} async-done(((bf16[1152,144]{0,1:T(8,128)(2,1)}), bf16[1152,1152]{0,1:T(8,128)(2,1)}) %all-gather.28.cloned.1.call-update) | async-done | bytes 2654224 | tf_op jit(solution)/shard_map/all_gather | solution.py:43
  476.6 38.3 %all-gather.26.cloned.1.call-done = bf16[2048,1152]{1,0:T(8,128)(2,1)} async-done(((bf16[512,1152]{1,0:T(8,128)(2,1)}), bf16[2048,1152]{1,0:T(8,128)(2,1)}) %all-gather.26.cloned.1.call-update) | async-done | bytes 4718608 | tf_op jit(solution)/shard_map/all_gather | solution.py:210
  514.9 16.0 %convert_reduce_fusion = (f32[1152]{0:T(1024)}, bf16[2048,1152]{1,0:T(8,128)(2,1)}) fusion(f32[2048,1152]{1,0:T(8,128)} %convolution_add_fusion, bf16[2048,1152]{1,0:T(8,128)(2,1)} %all-gather.26.cloned.1.call-done, bf16[1152,1152]{0,1:T(8,128)(2,1)} %all-gather.28.cloned.1.call-done), kind=kOutput, calls=%fused_computation.64 | convolution fusion | flops 5485362176 | bytes 21533184 | tf_op jit(solution)/shard_map/dot_general | solution.py:76
  530.9 41.5 %all-gather.30.cloned.1.call-done = bf16[1152,1152]{1,0:T(8,128)(2,1)} async-done(((bf16[144,1152]{1,0:T(8,128)(2,1)}), bf16[1152,1152]{1,0:T(8,128)(2,1)}) %all-gather.30.cloned.1.call-update) | async-done | bytes 2654224 | tf_op jit(solution)/shard_map/all_gather | solution.py:38
  572.3 11.0 convolution_convert_fusion.2
  583.8 44.4 %all-gather.24.cloned.1.call-done = bf16[1152,1152]{0,1:T(8,128)(2,1)} async-done(((bf16[1152,144]{0,1:T(8,128)(2,1)}), bf16[1152,1152]{0,1:T(8,128)(2,1)}) %all-gather.24.cloned.1.call-update) | async-done | bytes 2654224 | tf_op jit(solution)/shard_map/all_gather | solution.py:43
  628.2 13.0 convolution_convert_fusion.3
  642.0 35.4 %reduce-scatter.17.cloned.1.call-done = bf16[512,1152]{1,0:T(8,128)(2,1)} async-done(((bf16[2048,1152]{1,0:T(8,128)(2,1)}), bf16[512,1152]{1,0:T(8,128)(2,1)}) %reduce-scatter.17.cloned.1.call-update) | async-done | bytes 1179664 | tf_op jit(solution)/shard_map/reduce_scatter | solution.py:53
  680.9 46.8 %reduce-scatter.15.cloned.1.call-done = bf16[512,1152]{1,0:T(8,128)(2,1)} async-done(((bf16[2048,1152]{1,0:T(8,128)(2,1)}), bf16[512,1152]{1,0:T(8,128)(2,1)}) %reduce-scatter.15.cloned.1.call-update) | async-done | bytes 1179664 | tf_op jit(solution)/shard_map/reduce_scatter | solution.py:195
  727.7 7.9 convert_reduce_fusion.4
  735.6 32.4 %all_gather.57 = bf16[288,1152]{0,1:T(8,128)(2,1)S(1)} all-gather(bf16[288,144]{0,1:T(8,128)(2,1)S(1)} %copy-done.25), channel_id=1, replica_groups=mesh['dp'=8,'tensor'=4] {'dp'}, dimensions={1}, use_global_device_ids=true | all-gather | bytes 746496 | tf_op jit(solution)/shard_map/all_gather | solution.py:42
  768.1 5.1 all-gather.32.cloned.1.call-done
  773.2 5.1 convolution_convert_fusion.5
  778.3 4.1 reshape.217
  785.1 75.6 %while.23 = (s32[]{:T(128)}, bf16[2,1024,4,3,72]{1,4,2,3,0:T(8,128)(2,1)}, bf16[2,1024,4,72]{1,3,2,0:T(8,128)(2,1)S(1)}, bf16[2,1024,4,72]{1,3,2,0:T(8,128)(2,1)...) while((s32[]{:T(128)}, ...), condition=%wide.region_15.16_spmd, body=%wide.region_13.15_spmd.sunk | while | flops 3077009408 | bytes 199608528 | solution.py:225
  787.5 4.9 fusion.160
  792.5 9.2 multiply_reduce_fusion.7
  801.7 8.0 multiply_convert_fusion.7
  814.7 6.3 fusion.161
  825.3 4.9 fusion.160
  830.3 9.2 multiply_reduce_fusion.7
  839.5 7.9 multiply_convert_fusion.7
  852.4 6.2 fusion.161
  860.8 5.6 copy.81
  867.7 10.1 convolution_convert_fusion.1
  877.8 48.1 %reduce-scatter.19.cloned.1.call-done = bf16[512,1152]{1,0:T(8,128)(2,1)} async-done(((bf16[2048,1152]{1,0:T(8,128)(2,1)}), bf16[512,1152]{1,0:T(8,128)(2,1)}) %reduce-scatter.19.cloned.1.call-update) | async-done | bytes 1179664 | tf_op jit(solution)/shard_map/reduce_scatter | solution.py:53
  930.5 4.0 multiply_dynamic-update-slice_fusion
  938.4 4.8 convolution_convert_fusion
  946.1 14.2 fusion.95
  960.6 12.7 fusion.104
  973.4 6.8 fusion.103
  980.5 9.5 fusion.102
  990.7 5.6 fusion.88
  1000.2 49.2 %all-gather.36.cloned.1.call-done = bf16[1152,1728]{1,0:T(8,128)(2,1)} async-done(((bf16[144,1728]{1,0:T(8,128)(2,1)}), bf16[1152,1728]{1,0:T(8,128)(2,1)}) %all-gather.36.cloned.1.call-update) | async-done | bytes 3981328 | tf_op jit(solution)/shard_map/all_gather | solution.py:39
  1052.9 10.8 all-reduce.1
  1063.8 39.3 %all-reduce = (f32[1728]{0:T(1024)}, f32[576]{0:T(1024)}, f32[1152]{0:T(1024)}, f32[1152]{0:T(1024)}, f32[1152]{0:T(1024)}) all-reduce(f32[1728]{0:T(1024)S(1)} %convert_reduce_fusion.5, f32[576]{0:T(1024)S(1)} %reshape.219, f32[1152]{0:T(1024)S(1)} %get-tuple-element.178, ...), channel_id=1, replica_groups=mesh['dp'=8,'tensor'=4] {'dp'}, use_global_device_ids=true, to_apply=%region_23.24 | all-reduce | flops 5760 | bytes 46080 | tf_op jit(solution)/shard_map/psum | solution.py:257
  1103.1 54.5 %reduce-scatter.29.cloned.1.call-done = f32[1152,144]{0,1:T(8,128)} async-done(((f32[1152,1152]{0,1:T(8,128)}), f32[1152,144]{0,1:T(8,128)}) %reduce-scatter.29.cloned.1.call-update) | async-done | bytes 663568 | tf_op jit(solution)/shard_map/reduce_scatter | solution.py:267
  1157.7 108.1 %reduce-scatter.27.cloned.1.call-done = f32[144,1152]{1,0:T(8,128)} async-done(((f32[1152,1152]{1,0:T(8,128)}), f32[144,1152]{1,0:T(8,128)}) %reduce-scatter.27.cloned.1.call-update) | async-done | bytes 663568 | tf_op jit(solution)/shard_map/reduce_scatter | solution.py:262
  1265.8 70.3 %reduce-scatter.25.cloned.1.call-done = f32[288,144]{0,1:T(8,128)} async-done(((f32[288,1152]{0,1:T(8,128)}), f32[288,144]{0,1:T(8,128)}) %reduce-scatter.25.cloned.1.call-update) | async-done | bytes 165904 | tf_op jit(solution)/shard_map/reduce_scatter | solution.py:266
  1336.1 90.6 %reduce-scatter.23.cloned.1.call-done = f32[144,864]{1,0:T(8,128)} async-done(((f32[1152,864]{1,0:T(8,128)}), f32[144,864]{1,0:T(8,128)}) %reduce-scatter.23.cloned.1.call-update) | async-done | bytes 497680 | tf_op jit(solution)/shard_map/reduce_scatter | solution.py:261
  1426.7 151.3 %reduce-scatter.21.cloned.1.call-done = f32[144,1728]{1,0:T(8,128)} async-done(((f32[1152,1728]{1,0:T(8,128)}), f32[144,1728]{1,0:T(8,128)}) %reduce-scatter.21.cloned.1.call-update) | async-done | bytes 995344 | tf_op jit(solution)/shard_map/reduce_scatter | solution.py:263
  (222 shorter events, 84.4 us)
Async XLA Ops:
  7.2 3.8 copy-start.5
  7.2 78.3 %copy-start.35 = (bf16[2,1152]{1,0:T(2,128)(2,1)S(1)}, bf16[2,1152]{1,0:T(2,128)(2,1)}, u32[]{:S(2)}) copy-start(bf16[2,1152]{1,0:T(2,128)(2,1)} %param.18) | copy-start | bytes 13828
  7.2 78.3 %all-gather.14.cloned.1.call-start = ((), (), s32[]{:S(2)}) async-start(), calls=%async_computation.10 | async-start | bytes 4644864 | tf_op jit(solution)/shard_map/all_gather | solution.py:39
  7.9 139.1 %all-gather.18.cloned.1.call-start = ((), (), s32[]{:S(2)}) async-start(), calls=%async_computation.12 | async-start | bytes 2322432 | tf_op jit(solution)/shard_map/all_gather | solution.py:37
  8.7 177.7 %all-gather.16.cloned.1.call-start = ((), (), s32[]{:S(2)}) async-start(), calls=%async_computation.11 | async-start | bytes 5898240 | tf_op jit(solution)/shard_map/all_gather | solution.py:49
  9.4 84.3 %copy-start.27 = (s32[512]{0:T(512)}, s32[512]{0:T(512)S(1)}, u32[]{:S(2)}) copy-start(s32[512]{0:T(512)S(1)} %add_select_fusion) | copy-start | bytes 6148
  11.0 88.5 %copy-start.39 = (f32[512]{0:T(512)}, f32[512]{0:T(512)S(1)}, u32[]{:S(2)}) copy-start(f32[512]{0:T(512)S(1)} %broadcast_multiply_fusion.5) | copy-start | bytes 6148
  11.4 88.0 %copy-start.43 = (f32[512]{0:T(512)}, f32[512]{0:T(512)S(1)}, u32[]{:S(2)}) copy-start(f32[512]{0:T(512)S(1)} %add_rsqrt_fusion.1) | copy-start | bytes 6148
  99.5 5.0 copy-start.1
  104.5 1.8 copy-start.24
  106.1 217.6 %reduce-scatter.13.cloned.1.call-start = ((), (), s32[]{:S(2)}) async-start(), calls=%async_computation.13 | async-start | bytes 5898240 | tf_op jit(solution)/shard_map/reduce_scatter | solution.py:180
  210.3 5.6 copy-start.26
  224.2 8.7 copy-start.8
  224.2 8.7 copy-start.21
  249.8 8.7 copy-start.8
  249.8 8.7 copy-start.21
  267.3 3.9 copy-start.23
  275.7 105.3 %all-gather.22.cloned.1.call-start = ((), (), s32[]{:S(2)}) async-start(), calls=%async_computation.15 | async-start | bytes 2985984 | tf_op jit(solution)/shard_map/all_gather | solution.py:38
  276.3 142.9 %all-gather.20.cloned.1.call-start = ((), (), s32[]{:S(2)}) async-start(), calls=%async_computation.14 | async-start | bytes 5898240 | tf_op jit(solution)/shard_map/all_gather | solution.py:49
  276.6 50.0 %copy-start.29 = (f32[1152]{0:T(1024)}, f32[1152]{0:T(1024)S(1)}, u32[]{:S(2)}) copy-start(f32[1152]{0:T(1024)S(1)} %convert_element_type.141) | copy-start | bytes 13828
  326.6 7.8 copy-start.2
  326.6 2.1 copy-start.13
  326.6 401.0 %copy-start.33 = (f32[512]{0:T(512)}, f32[512]{0:T(512)S(1)}, u32[]{:S(2)}) copy-start(f32[512]{0:T(512)S(1)} %broadcast_multiply_fusion.4) | copy-start | bytes 6148
  328.7 398.9 %copy-start.37 = (f32[512]{0:T(512)}, f32[512]{0:T(512)S(1)}, u32[]{:S(2)}) copy-start(f32[512]{0:T(512)S(1)} %add_rsqrt_fusion) | copy-start | bytes 6148
  334.3 2.9 copy-start.47
  334.4 142.2 %all-gather.28.cloned.1.call-start = ((), (), s32[]{:S(2)}) async-start(), calls=%async_computation.19 | async-start | bytes 2985984 | tf_op jit(solution)/shard_map/all_gather | solution.py:43
  335.1 179.8 %all-gather.26.cloned.1.call-start = ((), (), s32[]{:S(2)}) async-start(), calls=%async_computation.18 | async-start | bytes 5898240 | tf_op jit(solution)/shard_map/all_gather | solution.py:210
  335.9 236.5 %all-gather.30.cloned.1.call-start = ((), (), s32[]{:S(2)}) async-start(), calls=%async_computation.20 | async-start | bytes 2985984 | tf_op jit(solution)/shard_map/all_gather | solution.py:38
  336.6 291.6 %all-gather.24.cloned.1.call-start = ((), (), s32[]{:S(2)}) async-start(), calls=%async_computation.16 | async-start | bytes 2985984 | tf_op jit(solution)/shard_map/all_gather | solution.py:43
  337.2 340.2 %reduce-scatter.17.cloned.1.call-start = ((), (), s32[]{:S(2)}) async-start(), calls=%async_computation.21 | async-start | bytes 5898240 | tf_op jit(solution)/shard_map/reduce_scatter | solution.py:53
  583.3 144.3 %reduce-scatter.15.cloned.1.call-start = ((), (), s32[]{:S(2)}) async-start(), calls=%async_computation.17 | async-start | bytes 5898240 | tf_op jit(solution)/shard_map/reduce_scatter | solution.py:195
  641.3 131.9 %all-gather.32.cloned.1.call-start = ((), (), s32[]{:S(2)}) async-start(), calls=%async_computation.22 | async-start | bytes 5898240 | tf_op jit(solution)/shard_map/all_gather | solution.py:222
  642.0 85.7 %copy-start.31 = (f32[1152]{0:T(1024)}, f32[1152]{0:T(1024)S(1)}, u32[]{:S(2)}) copy-start(f32[1152]{0:T(1024)S(1)} %convert_element_type.147) | copy-start | bytes 13828
  727.7 8.0 copy-start.25
  735.6 132.1 %all-gather.34.cloned.1.call-start = ((), (), s32[]{:S(2)}) async-start(), calls=%async_computation.23 | async-start | bytes 2322432 | tf_op jit(solution)/shard_map/all_gather | solution.py:37
  768.1 157.8 %reduce-scatter.19.cloned.1.call-start = ((), (), s32[]{:S(2)}) async-start(), calls=%async_computation.24 | async-start | bytes 5898240 | tf_op jit(solution)/shard_map/reduce_scatter | solution.py:53
  809.7 3.3 copy-start
  814.6 6.3 copy-start.4
  814.6 6.3 copy-start.9
  821.2 1.7 copy-start.10
  847.4 3.3 copy-start
  852.3 6.2 copy-start.4
  852.3 6.2 copy-start.9
  858.8 1.7 copy-start.10
  867.6 10.1 copy-start.18
  877.8 49.7 %copy-start.6 = (bf16[512,1152]{1,0:T(8,128)(2,1)S(1)}, bf16[512,1152]{1,0:T(8,128)(2,1)}, u32[]{:S(2)}) copy-start(bf16[512,1152]{1,0:T(8,128)(2,1)} %param.17) | copy-start | bytes 3538948
  877.8 49.7 %copy-start.40 = (f32[512]{0:T(512)S(1)}, f32[512]{0:T(512)}, u32[]{:S(2)}) copy-start(f32[512]{0:T(512)} %copy-done.39) | copy-start | bytes 6148
  877.8 49.7 %copy-start.44 = (f32[512]{0:T(512)S(1)}, f32[512]{0:T(512)}, u32[]{:S(2)}) copy-start(f32[512]{0:T(512)} %copy-done.43) | copy-start | bytes 6148
  877.8 112.3 %reduce-scatter.31.cloned.1.call-start = ((), (), s32[]{:S(2)}) async-start(), calls=%async_computation.31 | async-start | bytes 2211840
  927.5 2.9 copy-start.15
  927.5 2.9 copy-start.16
  927.5 2.9 copy-start.30
  930.5 4.0 copy-start.7
  945.0 104.4 %all-gather.36.cloned.1.call-start = ((), (), s32[]{:S(2)}) async-start(), calls=%async_computation.25 | async-start | bytes 4644864 | tf_op jit(solution)/shard_map/all_gather | solution.py:39
  945.6 212.1 %reduce-scatter.29.cloned.1.call-start = ((), (), s32[]{:S(2)}) async-start(), calls=%async_computation.30 | async-start | bytes 5971968 | tf_op jit(solution)/shard_map/reduce_scatter | solution.py:267
  960.3 305.5 %reduce-scatter.27.cloned.1.call-start = ((), (), s32[]{:S(2)}) async-start(), calls=%async_computation.29 | async-start | bytes 5971968 | tf_op jit(solution)/shard_map/reduce_scatter | solution.py:262
  973.3 7.1 copy-start.19
  973.3 362.8 %reduce-scatter.25.cloned.1.call-start = ((), (), s32[]{:S(2)}) async-start(), calls=%async_computation.28 | async-start | bytes 1990656 | tf_op jit(solution)/shard_map/reduce_scatter | solution.py:266
  980.2 446.5 %reduce-scatter.23.cloned.1.call-start = ((), (), s32[]{:S(2)}) async-start(), calls=%async_computation.27 | async-start | bytes 4644864 | tf_op jit(solution)/shard_map/reduce_scatter | solution.py:261
  990.0 588.0 %reduce-scatter.21.cloned.1.call-start = ((), (), s32[]{:S(2)}) async-start(), calls=%async_computation.26 | async-start | bytes 9289728 | tf_op jit(solution)/shard_map/reduce_scatter | solution.py:263
  996.2 2.0 copy-start.11
  998.8 54.1 %copy-start.41 = (f32[1152]{0:T(1024)S(1)}, f32[1152]{0:T(1024)}, u32[]{:S(2)}) copy-start(f32[1152]{0:T(1024)} %get-tuple-element.182) | copy-start | bytes 13828
  998.8 54.1 %copy-start.42 = (f32[1152]{0:T(1024)S(1)}, f32[1152]{0:T(1024)}, u32[]{:S(2)}) copy-start(f32[1152]{0:T(1024)} %get-tuple-element.180) | copy-start | bytes 13828
  998.9 64.9 %copy-start.45 = (f32[1152]{0:T(1024)S(1)}, f32[1152]{0:T(1024)}, u32[]{:S(2)}) copy-start(f32[1152]{0:T(1024)} %get-tuple-element.202) | copy-start | bytes 13828
  (15 other events, 18.8 us)
Sparse Core Ops, SparseCore 0:
  10.2 75.2 all-gather.13
  87.7 59.3 all-gather.17
  149.2 37.1 all-gather.15
  275.8 47.8 reduce-scatter.12
  326.0 55.0 all-gather.21
  383.1 36.0 all-gather.19
  421.5 55.0 all-gather.27
  478.8 36.0 all-gather.25
  517.3 55.0 all-gather.29
  574.6 53.5 all-gather.23
  630.9 46.3 reduce-scatter.16
  679.8 47.8 reduce-scatter.14
  735.7 37.4 all-gather.31
  775.5 48.9 all-gather.33
  877.9 47.9 reduce-scatter.18
  945.1 29.3 reduce-scatter.30
  976.8 72.5 all-gather.35
  1053.9 103.7 reduce-scatter.28
  1161.8 103.9 reduce-scatter.26
  1270.1 65.9 reduce-scatter.24
  1340.3 86.3 reduce-scatter.22
  1431.4 146.5 reduce-scatter.20
where the time goes:
time: 1590 us
  waiting for transfers between devices  1080 us (68%)
  matrix products  225 us (14%)
  blocking collectives  124 us (8%)
  other arithmetic  71.7 us (5%)
  local copies, waits for them, and re-layouts  64.6 us (4%)
    reduce_scatter x1, waiting for transfers between devices, shards(): lax.psum_scatter(grad_ada, 'dp', scatter_dimension=0, tiled=True)  151 us
    all_gather x2, waiting for transfers between devices, fetch_weights(): lax.all_gather(w_ada, 'dp', axis=0, tiled=True)  123 us
    reduce_scatter x1, waiting for transfers between devices, shards(): lax.psum_scatter(grad_fc1, 'dp', scatter_dimension=0, tiled=True)  108 us
    reduce_scatter x1, waiting for transfers between devices, shards(): lax.psum_scatter(grad_wqkv, 'dp', scatter_dimension=0, tiled=True)  90.6 us
    all_gather x2, waiting for transfers between devices, fetch_weights(): lax.all_gather(w_fc2, 'dp', axis=1, tiled=True)  90.3 us
    all_gather x2, waiting for transfers between devices, fetch_weights(): lax.all_gather(w_fc1, 'dp', axis=0, tiled=True)  85.2 us
    reduce_scatter x2, waiting for transfers between devices, sum_back(): lax.psum_scatter(row_term(jnp.int32(0), lax.axis_size('tensor') * row_cou...  83.5 us
    all_gather x2, waiting for transfers between devices, gather_rows(): return lax.all_gather(values, 'tensor', axis=0, tiled=True)  77.4 us
  transfers between devices with their start and end apart: 22, of which 20 were waited for; matrix products, arithmetic and copies ran while one was open for 14% of the time, Pallas kernels for 0%

commit v1 on v0

--- a/solution.py
+++ b/solution.py
@@ -11,6 +11,24 @@
 epsilon = 1e-06
 
 
+def gather_around(value, axis, dim):
+    ways, here, lap = (lax.axis_size(axis), lax.axis_index(axis), value.shape[dim])
+    shape = [n * ways if d == dim else n for d, n in enumerate(value.shape)]
+    full = lax.dynamic_update_slice_in_dim(
+        jnp.zeros(shape, value.dtype), value, here * lap, axis=dim
+    )
+    going_up = going_down = value
+    for far in range(1, ways // 2 + 1):
+        going_up = lax.ppermute(going_up, axis, [(d, (d + 1) % ways) for d in range(ways)])
+        full = lax.dynamic_update_slice_in_dim(full, going_up, (here - far) % ways * lap, axis=dim)
+        if 2 * far < ways:
+            going_down = lax.ppermute(going_down, axis, [(d, (d - 1) % ways) for d in range(ways)])
+            full = lax.dynamic_update_slice_in_dim(
+                full, going_down, (here + far) % ways * lap, axis=dim
+            )
+    return full
+
+
 def normalize(values):
     centre = values - jnp.mean(values, axis=-1, keepdims=True)
     inverse = lax.rsqrt(jnp.mean(centre * centre, axis=-1, keepdims=True) + epsilon)
@@ -36,7 +54,7 @@
     columns = (
         lax.all_gather(w_qkv, "dp", axis=0, tiled=True),
         lax.all_gather(w_fc1, "dp", axis=0, tiled=True),
-        lax.all_gather(w_ada, "dp", axis=0, tiled=True),
+        gather_around(w_ada, "dp", 0),
     )
     row_parts = (
         lax.all_gather(w_proj, "dp", axis=1, tiled=True),

time: 1590 us -> 1550 us (0.975)
  waiting for transfers between devices: 1080 us -> 981 us
  starting transfers between devices: 2.35 us -> 47 us
    ppermute x0 -> x14, waiting for transfers between devices: none -> 142 us  [the longest x8 118 us: gather_around(): lax.ppermute(going_up, axis, [(d, (d + 1) % ways) for d in range(ways)])]
    all_gather x2 -> x0, waiting for transfers between devices: 123 us -> none  [fetch_weights(): lax.all_gather(w_ada, 'dp', axis=0, tiled=True)]
    reduce_scatter x1, waiting for transfers between devices: 54.5 us -> 0.01 us  [shards(): lax.psum_scatter(grad_fc2, 'dp', scatter_dimension=1, tiled=True)]
    ppermute x0 -> x14, starting transfers between devices: none -> 44.7 us  [the longest x6 32.9 us: gather_around(): lax.ppermute(going_down, axis, [(d, (d - 1) % ways) for d in range(ways)])]
    all_gather x2, waiting for transfers between devices: 77.4 us -> 40.8 us  [gather_rows(): return lax.all_gather(values, 'tensor', axis=0, tiled=True)]
    reduce_scatter x1, waiting for transfers between devices: 108 us -> 85.4 us  [shards(): lax.psum_scatter(grad_fc1, 'dp', scatter_dimension=0, tiled=True)]
  transfers between devices with their start and end apart: 22 -> 34, of which waited for: 20 -> 27; matrix products, arithmetic and copies ran while one was open for 14% -> 15% of each run, Pallas kernels for 0% -> 0%
where the time goes in v1:
time: 1550 us
  waiting for transfers between devices  981 us (63%)
  matrix products  225 us (15%)
  blocking collectives  126 us (8%)
  local copies, waits for them, and re-layouts  77.6 us (5%)
  other arithmetic  72.9 us (5%)
  starting transfers between devices  47 us (3%)
    reduce_scatter x1, waiting for transfers between devices, shards(): lax.psum_scatter(grad_ada, 'dp', scatter_dimension=0, tiled=True)  151 us
    ppermute x8, waiting for transfers between devices, gather_around(): lax.ppermute(going_up, axis, [(d, (d + 1) % ways) for d in range(ways)])  118 us
    reduce_scatter x1, waiting for transfers between devices, shards(): lax.psum_scatter(grad_wqkv, 'dp', scatter_dimension=0, tiled=True)  90.7 us
    all_gather x2, waiting for transfers between devices, fetch_weights(): lax.all_gather(w_fc2, 'dp', axis=1, tiled=True)  90.3 us
    all_gather x2, waiting for transfers between devices, fetch_weights(): lax.all_gather(w_fc1, 'dp', axis=0, tiled=True)  86.5 us
    reduce_scatter x1, waiting for transfers between devices, shards(): lax.psum_scatter(grad_fc1, 'dp', scatter_dimension=0, tiled=True)  85.4 us
    reduce_scatter x2, waiting for transfers between devices, sum_back(): lax.psum_scatter(row_term(jnp.int32(0), lax.axis_size('tensor') * row_cou...  83.4 us
    reduce_scatter x1, waiting for transfers between devices, shards(): lax.psum_scatter(grad_proj, 'dp', scatter_dimension=1, tiled=True)  70.4 us
  transfers between devices with their start and end apart: 34, of which 27 were waited for; matrix products, arithmetic and copies ran while one was open for 15% of the time, Pallas kernels for 0%

profile of v1, /device:TPU:0, one launch (start us, length us, event | category | flops | bytes accessed | tf_op | source)
XLA Modules:
  0.0 1545.4 jit_solution(14119779915899425024)
XLA Ops:
  18.0 17.4 %collective-permute-done = bf16[144,1728]{1,0:T(8,128)(2,1)S(1)} collective-permute-done((bf16[144,1728]{1,0:T(8,128)(2,1)}, bf16[144,1728]{1,0:T(8,128)(2,1)S(1)}, u32[]{:S(2)}, u32[]{:S(2)}) %collective-permute-start) | collective-permute-done | bytes 497696 | tf_op jit(solution)/shard_map/ppermute | solution.py:22
  41.6 29.5 %collective-permute-done.2 = bf16[144,1728]{1,0:T(8,128)(2,1)S(1)} collective-permute-done((bf16[144,1728]{1,0:T(8,128)(2,1)S(1)}, bf16[144,1728]{1,0:T(8,128)(2,1)S(1)}, u32[]{:S(2)}, u32[]{:S(2)}) %collective-permute-start.2) | collective-permute-done | bytes 497696 | tf_op jit(solution)/shard_map/ppermute | solution.py:22
  75.2 5.3 collective-permute-done.3
  81.3 10.3 collective-permute-done.4
  93.3 12.8 collective-permute-done.5
  110.5 5.2 all-gather
  115.9 5.7 fusion.77
  121.7 5.0 copy-done.1
  128.5 35.4 %all_gather.42 = bf16[288,1152]{0,1:T(8,128)(2,1)} all-gather(bf16[288,144]{0,1:T(8,128)(2,1)S(1)} %copy-done.27), channel_id=1, replica_groups=mesh['dp'=8,'tensor'=4] {'dp'}, dimensions={1}, use_global_device_ids=true | all-gather | bytes 746496 | tf_op jit(solution)/shard_map/all_gather | solution.py:60
  166.6 7.4 fusion.101
  196.1 51.5 %while.22 = (s32[]{:T(128)}, bf16[2,1024,4,72]{1,3,2,0:T(8,128)(2,1)}, f32[2,4,1024]{2,1,0:T(4,128)}, bf16[2,1024,4,72]{1,3,2,0:T(8,128)(2,1)}, bf16[2,1024,4,72...) while((s32[]{:T(128)}, bf16[2,1024,4,72]{1,3,2,0:T(8,128)(2,1)}, ...), condition=%wide.region_5.6_spmd, body=%wide.region_2.5_spmd.sunk | while | flops 1245999104 | bytes 66980012 | solution.py:196
  196.3 8.2 multiply_reduce_fusion.6
  204.5 8.7 fusion.149
  213.2 7.7 fusion.150
  221.9 8.2 multiply_reduce_fusion.6
  230.1 8.7 fusion.149
  238.8 7.7 fusion.150
  256.9 47.1 %reduce-scatter.13.cloned.1.call-done = bf16[512,1152]{1,0:T(8,128)(2,1)} async-done(((bf16[2048,1152]{1,0:T(8,128)(2,1)}), bf16[512,1152]{1,0:T(8,128)(2,1)}) %reduce-scatter.13.cloned.1.call-update) | async-done | bytes 1179664 | tf_op jit(solution)/shard_map/reduce_scatter | solution.py:198
  307.4 6.0 convert_reduce_fusion.3
  316.3 45.0 %all-gather.18.cloned.1.call-done = bf16[1152,1152]{1,0:T(8,128)(2,1)} async-done(((bf16[144,1152]{1,0:T(8,128)(2,1)}), bf16[1152,1152]{1,0:T(8,128)(2,1)}) %all-gather.18.cloned.1.call-update) | async-done | bytes 2654224 | tf_op jit(solution)/shard_map/all_gather | solution.py:56
  361.3 38.1 %all-gather.16.cloned.1.call-done = bf16[2048,1152]{1,0:T(8,128)(2,1)} async-done(((bf16[512,1152]{1,0:T(8,128)(2,1)}), bf16[2048,1152]{1,0:T(8,128)(2,1)}) %all-gather.16.cloned.1.call-update) | async-done | bytes 4718608 | tf_op jit(solution)/shard_map/all_gather | solution.py:67
  399.4 11.6 convolution_add_fusion
  411.0 45.7 %all-gather.24.cloned.1.call-done = bf16[1152,1152]{0,1:T(8,128)(2,1)} async-done(((bf16[1152,144]{0,1:T(8,128)(2,1)}), bf16[1152,1152]{0,1:T(8,128)(2,1)}) %all-gather.24.cloned.1.call-update) | async-done | bytes 2654224 | tf_op jit(solution)/shard_map/all_gather | solution.py:61
  456.7 38.3 %all-gather.22.cloned.1.call-done = bf16[2048,1152]{1,0:T(8,128)(2,1)} async-done(((bf16[512,1152]{1,0:T(8,128)(2,1)}), bf16[2048,1152]{1,0:T(8,128)(2,1)}) %all-gather.22.cloned.1.call-update) | async-done | bytes 4718608 | tf_op jit(solution)/shard_map/all_gather | solution.py:228
  495.0 16.0 %convert_reduce_fusion = (f32[1152]{0:T(1024)}, bf16[2048,1152]{1,0:T(8,128)(2,1)}) fusion(f32[2048,1152]{1,0:T(8,128)} %convolution_add_fusion, bf16[2048,1152]{1,0:T(8,128)(2,1)} %all-gather.22.cloned.1.call-done, bf16[1152,1152]{0,1:T(8,128)(2,1)} %all-gather.24.cloned.1.call-done), kind=kOutput, calls=%fused_computation.64 | convolution fusion | flops 5485362176 | bytes 21533184 | tf_op jit(solution)/shard_map/dot_general | solution.py:94
  511.0 41.5 %all-gather.26.cloned.1.call-done = bf16[1152,1152]{1,0:T(8,128)(2,1)} async-done(((bf16[144,1152]{1,0:T(8,128)(2,1)}), bf16[1152,1152]{1,0:T(8,128)(2,1)}) %all-gather.26.cloned.1.call-update) | async-done | bytes 2654224 | tf_op jit(solution)/shard_map/all_gather | solution.py:56
  552.5 11.0 convolution_convert_fusion.2
  564.0 44.6 %all-gather.20.cloned.1.call-done = bf16[1152,1152]{0,1:T(8,128)(2,1)} async-done(((bf16[1152,144]{0,1:T(8,128)(2,1)}), bf16[1152,1152]{0,1:T(8,128)(2,1)}) %all-gather.20.cloned.1.call-update) | async-done | bytes 2654224 | tf_op jit(solution)/shard_map/all_gather | solution.py:61
  608.5 13.0 convolution_convert_fusion.3
  622.3 35.3 %reduce-scatter.17.cloned.1.call-done = bf16[512,1152]{1,0:T(8,128)(2,1)} async-done(((bf16[2048,1152]{1,0:T(8,128)(2,1)}), bf16[512,1152]{1,0:T(8,128)(2,1)}) %reduce-scatter.17.cloned.1.call-update) | async-done | bytes 1179664 | tf_op jit(solution)/shard_map/reduce_scatter | solution.py:71
  661.1 46.9 %reduce-scatter.15.cloned.1.call-done = bf16[512,1152]{1,0:T(8,128)(2,1)} async-done(((bf16[2048,1152]{1,0:T(8,128)(2,1)}), bf16[512,1152]{1,0:T(8,128)(2,1)}) %reduce-scatter.15.cloned.1.call-update) | async-done | bytes 1179664 | tf_op jit(solution)/shard_map/reduce_scatter | solution.py:213
  707.9 7.9 convert_reduce_fusion.4
  715.9 32.4 %all_gather.50 = bf16[288,1152]{0,1:T(8,128)(2,1)S(1)} all-gather(bf16[288,144]{0,1:T(8,128)(2,1)S(1)} %copy-done.28), channel_id=1, replica_groups=mesh['dp'=8,'tensor'=4] {'dp'}, dimensions={1}, use_global_device_ids=true | all-gather | bytes 746496 | tf_op jit(solution)/shard_map/all_gather | solution.py:60
  748.4 5.0 all-gather.28.cloned.1.call-done
  753.5 5.1 convolution_convert_fusion.5
  765.4 75.8 %while.23 = (s32[]{:T(128)}, bf16[2,1024,4,3,72]{1,4,2,3,0:T(8,128)(2,1)}, bf16[2,1024,4,72]{1,3,2,0:T(8,128)(2,1)S(1)}, bf16[2,1024,4,72]{1,3,2,0:T(8,128)(2,1)...) while((s32[]{:T(128)}, ...), condition=%wide.region_15.16_spmd, body=%wide.region_13.15_spmd.sunk | while | flops 3077009408 | bytes 199608528 | solution.py:243
  767.8 4.9 fusion.160
  772.7 9.2 multiply_reduce_fusion.7
  782.0 8.1 multiply_convert_fusion.7
  795.0 6.3 fusion.161
  805.7 4.9 fusion.160
  810.6 9.2 multiply_reduce_fusion.7
  819.9 7.9 multiply_convert_fusion.7
  832.8 6.2 fusion.161
  841.2 5.6 copy.81
  848.1 10.1 convolution_convert_fusion.1
  858.3 48.1 %reduce-scatter.19.cloned.1.call-done = bf16[512,1152]{1,0:T(8,128)(2,1)} async-done(((bf16[2048,1152]{1,0:T(8,128)(2,1)}), bf16[512,1152]{1,0:T(8,128)(2,1)}) %reduce-scatter.19.cloned.1.call-update) | async-done | bytes 1179664 | tf_op jit(solution)/shard_map/reduce_scatter | solution.py:71
  918.9 4.8 convolution_convert_fusion
  925.9 14.0 fusion.95
  940.2 12.7 fusion.104
  953.0 6.8 fusion.103
  960.1 9.5 fusion.102
  970.3 5.6 fusion.88
  981.6 23.3 %collective-permute-done.7 = bf16[144,1728]{1,0:T(8,128)(2,1)S(1)} collective-permute-done((bf16[144,1728]{1,0:T(8,128)(2,1)S(1)}, bf16[144,1728]{1,0:T(8,128)(2,1)S(1)}, u32[]{:S(2)}, u32[]{:S(2)}) %collective-permute-start.7) | collective-permute-done | bytes 497696 | tf_op jit(solution)/shard_map/ppermute | solution.py:22
  1014.8 19.4 %collective-permute-done.9 = bf16[144,1728]{1,0:T(8,128)(2,1)S(1)} collective-permute-done((bf16[144,1728]{1,0:T(8,128)(2,1)S(1)}, bf16[144,1728]{1,0:T(8,128)(2,1)S(1)}, u32[]{:S(2)}, u32[]{:S(2)}) %collective-permute-start.9) | collective-permute-done | bytes 497696 | tf_op jit(solution)/shard_map/ppermute | solution.py:22
  1037.9 20.4 %collective-permute-start.12 = (bf16[144,1728]{1,0:T(8,128)(2,1)S(1)}, bf16[144,1728]{1,0:T(8,128)(2,1)S(1)}, u32[]{:S(2)}, u32[]{:S(2)}) collective-permute-start(bf16[144,1728]{1,0:T(8,128)(2,1)S(1)} %collective-permute-done.10), channel_id=1, source_target_pairs={{0,28},{4,0},{8,4},{12,8},{16,12},{20,16},{24,20},{28,24},{1,29},{... | collective-permute-start | bytes 1493000 | tf_op jit(solution)/shard_map/ppermute | solution.py:25
  1059.2 7.7 collective-permute-done.11
  1071.9 10.7 collective-permute-done.13
  1087.7 11.4 all-reduce.1
  1099.1 41.5 %all-reduce = (f32[1728]{0:T(1024)}, f32[576]{0:T(1024)}, f32[1152]{0:T(1024)}, f32[1152]{0:T(1024)}, f32[1152]{0:T(1024)}) all-reduce(f32[1728]{0:T(1024)S(1)} %convert_reduce_fusion.5, f32[576]{0:T(1024)S(1)} %reshape.219, f32[1152]{0:T(1024)S(1)} %get-tuple-element.178, ...), channel_id=1, replica_groups=mesh['dp'=8,'tensor'=4] {'dp'}, use_global_device_ids=true, to_apply=%region_23.24 | all-reduce | flops 5760 | bytes 46080 | tf_op jit(solution)/shard_map/psum | solution.py:275
  1140.7 85.4 %reduce-scatter.27.cloned.1.call-done = f32[144,1152]{1,0:T(8,128)} async-done(((f32[1152,1152]{1,0:T(8,128)}), f32[144,1152]{1,0:T(8,128)}) %reduce-scatter.27.cloned.1.call-update) | async-done | bytes 663568 | tf_op jit(solution)/shard_map/reduce_scatter | solution.py:280
  1226.1 70.4 %reduce-scatter.25.cloned.1.call-done = f32[288,144]{0,1:T(8,128)} async-done(((f32[288,1152]{0,1:T(8,128)}), f32[288,144]{0,1:T(8,128)}) %reduce-scatter.25.cloned.1.call-update) | async-done | bytes 165904 | tf_op jit(solution)/shard_map/reduce_scatter | solution.py:284
  1296.5 90.7 %reduce-scatter.23.cloned.1.call-done = f32[144,864]{1,0:T(8,128)} async-done(((f32[1152,864]{1,0:T(8,128)}), f32[144,864]{1,0:T(8,128)}) %reduce-scatter.23.cloned.1.call-update) | async-done | bytes 497680 | tf_op jit(solution)/shard_map/reduce_scatter | solution.py:279
  1387.2 151.2 %reduce-scatter.21.cloned.1.call-done = f32[144,1728]{1,0:T(8,128)} async-done(((f32[1152,1728]{1,0:T(8,128)}), f32[144,1728]{1,0:T(8,128)}) %reduce-scatter.21.cloned.1.call-update) | async-done | bytes 995344 | tf_op jit(solution)/shard_map/reduce_scatter | solution.py:281
  (270 shorter events, 149.5 us)
Async XLA Ops:
  7.2 10.0 copy-start.21
  7.2 30.6 %copy-start.5 = (bf16[512,1152]{1,0:T(8,128)(2,1)S(1)}, bf16[512,1152]{1,0:T(8,128)(2,1)}, u32[]{:S(2)}) copy-start(bf16[512,1152]{1,0:T(8,128)(2,1)} %param.17) | copy-start | bytes 3538948
  7.2 156.7 %all-gather.14.cloned.1.call-start = ((), (), s32[]{:S(2)}) async-start(), calls=%async_computation.11 | async-start | bytes 2322432 | tf_op jit(solution)/shard_map/all_gather | solution.py:55
  7.2 28.1 %collective-permute-start = (bf16[144,1728]{1,0:T(8,128)(2,1)}, bf16[144,1728]{1,0:T(8,128)(2,1)S(1)}, u32[]{:S(2)}, u32[]{:S(2)}) collective-permute-start(bf16[144,1728]{1,0:T(8,128)(2,1)} %param.19), channel_id=1, source_target_pairs={{0,4},{4,8},{8,12},{12,16},{16,20},{20,24},{24,28},{28,0},{1,5},{5... | collective-permute-start | bytes 1493000 | tf_op jit(solution)/shard_map/ppermute | solution.py:22
  10.2 28.0 %collective-permute-start.1 = (bf16[144,1728]{1,0:T(8,128)(2,1)}, bf16[144,1728]{1,0:T(8,128)(2,1)S(1)}, u32[]{:S(2)}, u32[]{:S(2)}) collective-permute-start(bf16[144,1728]{1,0:T(8,128)(2,1)} %param.19), channel_id=1, source_target_pairs={{0,28},{4,0},{8,4},{12,8},{16,12},{20,16},{24,20},{28,24},{1,29},{... | collective-permute-start | bytes 1493000 | tf_op jit(solution)/shard_map/ppermute | solution.py:25
  13.4 153.2 %all-gather.12.cloned.1.call-start = ((), (), s32[]{:S(2)}) async-start(), calls=%async_computation.10 | async-start | bytes 5898240 | tf_op jit(solution)/shard_map/all_gather | solution.py:67
  14.9 26.6 %copy-start.49 = (bf16[1728]{0:T(1024)(128)(2,1)S(1)}, bf16[1728]{0:T(1024)(128)(2,1)}, u32[]{:S(2)}) copy-start(bf16[1728]{0:T(1024)(128)(2,1)} %param.20) | copy-start | bytes 10372
  18.0 103.6 %copy-start.42 = (f32[512]{0:T(512)}, f32[512]{0:T(512)S(1)}, u32[]{:S(2)}) copy-start(f32[512]{0:T(512)S(1)} %broadcast_multiply_fusion.5) | copy-start | bytes 6148
  35.4 35.7 %collective-permute-start.2 = (bf16[144,1728]{1,0:T(8,128)(2,1)S(1)}, bf16[144,1728]{1,0:T(8,128)(2,1)S(1)}, u32[]{:S(2)}, u32[]{:S(2)}) collective-permute-start(bf16[144,1728]{1,0:T(8,128)(2,1)S(1)} %collective-permute-done), channel_id=1, source_target_pairs={{0,4},{4,8},{8,12},{12,16},{16,20},{20,24},{24,28},{28,0},{1,5},{5... | collective-permute-start | bytes 1493000 | tf_op jit(solution)/shard_map/ppermute | solution.py:22
  38.2 83.4 %copy-start.46 = (f32[512]{0:T(512)}, f32[512]{0:T(512)S(1)}, u32[]{:S(2)}) copy-start(f32[512]{0:T(512)S(1)} %add_rsqrt_fusion.1) | copy-start | bytes 6148
  38.2 42.3 %collective-permute-start.3 = (bf16[144,1728]{1,0:T(8,128)(2,1)S(1)}, bf16[144,1728]{1,0:T(8,128)(2,1)S(1)}, u32[]{:S(2)}, u32[]{:S(2)}) collective-permute-start(bf16[144,1728]{1,0:T(8,128)(2,1)S(1)} %collective-permute-done.1), channel_id=1, source_target_pairs={{0,28},{4,0},{8,4},{12,8},{16,12},{20,16},{24,20},{28,24},{1,29},{... | collective-permute-start | bytes 1493000 | tf_op jit(solution)/shard_map/ppermute | solution.py:25
  41.4 74.6 %copy-start.30 = (s32[512]{0:T(512)}, s32[512]{0:T(512)S(1)}, u32[]{:S(2)}) copy-start(s32[512]{0:T(512)S(1)} %add_select_fusion) | copy-start | bytes 6148
  41.5 66.2 %copy-start.38 = (bf16[2,1152]{1,0:T(2,128)(2,1)S(1)}, bf16[2,1152]{1,0:T(2,128)(2,1)}, u32[]{:S(2)}) copy-start(bf16[2,1152]{1,0:T(2,128)(2,1)} %param.18) | copy-start | bytes 13828
  71.1 20.5 %collective-permute-start.4 = (bf16[144,1728]{1,0:T(8,128)(2,1)S(1)}, bf16[144,1728]{1,0:T(8,128)(2,1)S(1)}, u32[]{:S(2)}, u32[]{:S(2)}) collective-permute-start(bf16[144,1728]{1,0:T(8,128)(2,1)S(1)} %collective-permute-done.2), channel_id=1, source_target_pairs={{0,4},{4,8},{8,12},{12,16},{16,20},{20,24},{24,28},{28,0},{1,5},{5... | collective-permute-start | bytes 1493000 | tf_op jit(solution)/shard_map/ppermute | solution.py:22
  80.5 25.5 %collective-permute-start.5 = (bf16[144,1728]{1,0:T(8,128)(2,1)S(1)}, bf16[144,1728]{1,0:T(8,128)(2,1)S(1)}, u32[]{:S(2)}, u32[]{:S(2)}) collective-permute-start(bf16[144,1728]{1,0:T(8,128)(2,1)S(1)} %collective-permute-done.3), channel_id=1, source_target_pairs={{0,28},{4,0},{8,4},{12,8},{16,12},{20,16},{24,20},{28,24},{1,29},{... | collective-permute-start | bytes 1493000 | tf_op jit(solution)/shard_map/ppermute | solution.py:25
  91.6 15.3 collective-permute-start.6
  128.3 175.7 %reduce-scatter.13.cloned.1.call-start = ((), (), s32[]{:S(2)}) async-start(), calls=%async_computation.12 | async-start | bytes 5898240 | tf_op jit(solution)/shard_map/reduce_scatter | solution.py:198
  204.5 8.7 copy-start.8
  204.5 8.7 copy-start.24
  230.1 8.7 copy-start.8
  230.1 8.7 copy-start.24
  256.0 105.3 %all-gather.18.cloned.1.call-start = ((), (), s32[]{:S(2)}) async-start(), calls=%async_computation.14 | async-start | bytes 2985984 | tf_op jit(solution)/shard_map/all_gather | solution.py:56
  256.6 142.9 %all-gather.16.cloned.1.call-start = ((), (), s32[]{:S(2)}) async-start(), calls=%async_computation.13 | async-start | bytes 5898240 | tf_op jit(solution)/shard_map/all_gather | solution.py:67
  256.8 50.1 %copy-start.32 = (f32[1152]{0:T(1024)}, f32[1152]{0:T(1024)S(1)}, u32[]{:S(2)}) copy-start(f32[1152]{0:T(1024)S(1)} %convert_element_type.141) | copy-start | bytes 13828
  307.0 6.5 copy-start.2
  307.0 401.0 %copy-start.36 = (f32[512]{0:T(512)}, f32[512]{0:T(512)S(1)}, u32[]{:S(2)}) copy-start(f32[512]{0:T(512)S(1)} %broadcast_multiply_fusion.4) | copy-start | bytes 6148
  307.4 400.6 %copy-start.40 = (f32[512]{0:T(512)}, f32[512]{0:T(512)S(1)}, u32[]{:S(2)}) copy-start(f32[512]{0:T(512)S(1)} %add_rsqrt_fusion) | copy-start | bytes 6148
  307.4 8.9 copy-start.51
  313.4 143.3 %all-gather.24.cloned.1.call-start = ((), (), s32[]{:S(2)}) async-start(), calls=%async_computation.18 | async-start | bytes 2985984 | tf_op jit(solution)/shard_map/all_gather | solution.py:61
  314.0 181.0 %all-gather.22.cloned.1.call-start = ((), (), s32[]{:S(2)}) async-start(), calls=%async_computation.17 | async-start | bytes 5898240 | tf_op jit(solution)/shard_map/all_gather | solution.py:228
  314.8 237.7 %all-gather.26.cloned.1.call-start = ((), (), s32[]{:S(2)}) async-start(), calls=%async_computation.19 | async-start | bytes 2985984 | tf_op jit(solution)/shard_map/all_gather | solution.py:56
  315.5 293.0 %all-gather.20.cloned.1.call-start = ((), (), s32[]{:S(2)}) async-start(), calls=%async_computation.15 | async-start | bytes 2985984 | tf_op jit(solution)/shard_map/all_gather | solution.py:61
  316.3 341.3 %reduce-scatter.17.cloned.1.call-start = ((), (), s32[]{:S(2)}) async-start(), calls=%async_computation.20 | async-start | bytes 5898240 | tf_op jit(solution)/shard_map/reduce_scatter | solution.py:71
  563.5 144.4 %reduce-scatter.15.cloned.1.call-start = ((), (), s32[]{:S(2)}) async-start(), calls=%async_computation.16 | async-start | bytes 5898240 | tf_op jit(solution)/shard_map/reduce_scatter | solution.py:213
  621.6 131.9 %all-gather.28.cloned.1.call-start = ((), (), s32[]{:S(2)}) async-start(), calls=%async_computation.21 | async-start | bytes 5898240 | tf_op jit(solution)/shard_map/all_gather | solution.py:240
  622.3 93.6 %copy-start.34 = (f32[1152]{0:T(1024)}, f32[1152]{0:T(1024)S(1)}, u32[]{:S(2)}) copy-start(f32[1152]{0:T(1024)S(1)} %convert_element_type.147) | copy-start | bytes 13828
  707.9 8.0 copy-start.28
  715.8 132.2 %all-gather.30.cloned.1.call-start = ((), (), s32[]{:S(2)}) async-start(), calls=%async_computation.22 | async-start | bytes 2322432 | tf_op jit(solution)/shard_map/all_gather | solution.py:55
  748.4 158.0 %reduce-scatter.19.cloned.1.call-start = ((), (), s32[]{:S(2)}) async-start(), calls=%async_computation.23 | async-start | bytes 5898240 | tf_op jit(solution)/shard_map/reduce_scatter | solution.py:71
  758.6 6.8 copy-start.29
  795.0 6.3 copy-start.4
  795.0 6.3 copy-start.9
  832.7 6.2 copy-start.4
  848.0 10.1 copy-start.19
  858.2 49.7 %copy-start.6 = (bf16[512,1152]{1,0:T(8,128)(2,1)S(1)}, bf16[512,1152]{1,0:T(8,128)(2,1)}, u32[]{:S(2)}) copy-start(bf16[512,1152]{1,0:T(8,128)(2,1)} %param.17) | copy-start | bytes 3538948
  858.2 49.7 %copy-start.43 = (f32[512]{0:T(512)S(1)}, f32[512]{0:T(512)}, u32[]{:S(2)}) copy-start(f32[512]{0:T(512)} %copy-done.42) | copy-start | bytes 6148
  858.2 49.7 %copy-start.47 = (f32[512]{0:T(512)S(1)}, f32[512]{0:T(512)}, u32[]{:S(2)}) copy-start(f32[512]{0:T(512)} %copy-done.46) | copy-start | bytes 6148
  858.2 111.5 %reduce-scatter.31.cloned.1.call-start = ((), (), s32[]{:S(2)}) async-start(), calls=%async_computation.29 | async-start | bytes 2211840
  925.4 215.2 %reduce-scatter.29.cloned.1.call-start = ((), (), s32[]{:S(2)}) async-start(), calls=%async_computation.28 | async-start | bytes 5971968 | tf_op jit(solution)/shard_map/reduce_scatter | solution.py:285
  940.0 286.1 %reduce-scatter.27.cloned.1.call-start = ((), (), s32[]{:S(2)}) async-start(), calls=%async_computation.27 | async-start | bytes 5971968 | tf_op jit(solution)/shard_map/reduce_scatter | solution.py:280
  952.9 7.2 copy-start.20
  953.0 343.5 %reduce-scatter.25.cloned.1.call-start = ((), (), s32[]{:S(2)}) async-start(), calls=%async_computation.26 | async-start | bytes 1990656 | tf_op jit(solution)/shard_map/reduce_scatter | solution.py:284
  959.9 427.3 %reduce-scatter.23.cloned.1.call-start = ((), (), s32[]{:S(2)}) async-start(), calls=%async_computation.25 | async-start | bytes 4644864 | tf_op jit(solution)/shard_map/reduce_scatter | solution.py:279
  969.6 568.8 %reduce-scatter.21.cloned.1.call-start = ((), (), s32[]{:S(2)}) async-start(), calls=%async_computation.24 | async-start | bytes 9289728 | tf_op jit(solution)/shard_map/reduce_scatter | solution.py:281
  976.9 28.1 %collective-permute-start.7 = (bf16[144,1728]{1,0:T(8,128)(2,1)S(1)}, bf16[144,1728]{1,0:T(8,128)(2,1)S(1)}, u32[]{:S(2)}, u32[]{:S(2)}) collective-permute-start(bf16[144,1728]{1,0:T(8,128)(2,1)S(1)} %copy-done.22), channel_id=1, source_target_pairs={{0,4},{4,8},{8,12},{12,16},{16,20},{20,24},{24,28},{28,0},{1,5},{5... | collective-permute-start | bytes 1493000 | tf_op jit(solution)/shard_map/ppermute | solution.py:22
  978.4 30.2 %collective-permute-start.8 = (bf16[144,1728]{1,0:T(8,128)(2,1)S(1)}, bf16[144,1728]{1,0:T(8,128)(2,1)S(1)}, u32[]{:S(2)}, u32[]{:S(2)}) collective-permute-start(bf16[144,1728]{1,0:T(8,128)(2,1)S(1)} %copy-done.22), channel_id=1, source_target_pairs={{0,28},{4,0},{8,4},{12,8},{16,12},{20,16},{24,20},{28,24},{1,29},{... | collective-permute-start | bytes 1493000 | tf_op jit(solution)/shard_map/ppermute | solution.py:25
  1005.0 29.2 %collective-permute-start.9 = (bf16[144,1728]{1,0:T(8,128)(2,1)S(1)}, bf16[144,1728]{1,0:T(8,128)(2,1)S(1)}, u32[]{:S(2)}, u32[]{:S(2)}) collective-permute-start(bf16[144,1728]{1,0:T(8,128)(2,1)S(1)} %collective-permute-done.7), channel_id=1, source_target_pairs={{0,4},{4,8},{8,12},{12,16},{16,20},{20,24},{24,28},{28,0},{1,5},{5... | collective-permute-start | bytes 1493000 | tf_op jit(solution)/shard_map/ppermute | solution.py:22
  1008.6 29.3 %collective-permute-start.10 = (bf16[144,1728]{1,0:T(8,128)(2,1)S(1)}, bf16[144,1728]{1,0:T(8,128)(2,1)S(1)}, u32[]{:S(2)}, u32[]{:S(2)}) collective-permute-start(bf16[144,1728]{1,0:T(8,128)(2,1)S(1)} %collective-permute-done.8), channel_id=1, source_target_pairs={{0,28},{4,0},{8,4},{12,8},{16,12},{20,16},{24,20},{28,24},{1,29},{... | collective-permute-start | bytes 1493000 | tf_op jit(solution)/shard_map/ppermute | solution.py:25
  1014.7 68.7 %copy-start.11 = (bf16[2,1024,4,3,72]{1,4,2,3,0:T(8,128)(2,1)S(1)}, bf16[2,1024,4,3,72]{1,4,2,3,0:T(8,128)(2,1)}, u32[]{:S(2)}) copy-start(bf16[2,1024,4,3,72]{1,4,2,3,0:T(8,128)(2,1)} %get-tuple-element.93) | copy-start | bytes 10616836
  1034.1 32.7 %collective-permute-start.11 = (bf16[144,1728]{1,0:T(8,128)(2,1)S(1)}, bf16[144,1728]{1,0:T(8,128)(2,1)S(1)}, u32[]{:S(2)}, u32[]{:S(2)}) collective-permute-start(bf16[144,1728]{1,0:T(8,128)(2,1)S(1)} %collective-permute-done.9), channel_id=1, source_target_pairs={{0,4},{4,8},{8,12},{12,16},{16,20},{20,24},{24,28},{28,0},{1,5},{5... | collective-permute-start | bytes 1493000 | tf_op jit(solution)/shard_map/ppermute | solution.py:22
  1037.9 33.2 %collective-permute-start.12 = (bf16[144,1728]{1,0:T(8,128)(2,1)S(1)}, bf16[144,1728]{1,0:T(8,128)(2,1)S(1)}, u32[]{:S(2)}, u32[]{:S(2)}) collective-permute-start(bf16[144,1728]{1,0:T(8,128)(2,1)S(1)} %collective-permute-done.10), channel_id=1, source_target_pairs={{0,28},{4,0},{8,4},{12,8},{16,12},{20,16},{24,20},{28,24},{1,29},{... | collective-permute-start | bytes 1493000 | tf_op jit(solution)/shard_map/ppermute | solution.py:25
  1066.9 15.7 %collective-permute-start.13 = (bf16[144,1728]{1,0:T(8,128)(2,1)S(1)}, bf16[144,1728]{1,0:T(8,128)(2,1)S(1)}, u32[]{:S(2)}, u32[]{:S(2)}) collective-permute-start(bf16[144,1728]{1,0:T(8,128)(2,1)S(1)} %collective-permute-done.11), channel_id=1, source_target_pairs={{0,4},{4,8},{8,12},{12,16},{16,20},{20,24},{24,28},{28,0},{1,5},{5... | collective-permute-start | bytes 1493000 | tf_op jit(solution)/shard_map/ppermute | solution.py:22
  1070.2 13.9 copy-start.18
  1083.4 15.7 %copy-start.48 = (f32[1152]{0:T(1024)S(1)}, f32[1152]{0:T(1024)}, u32[]{:S(2)}) copy-start(f32[1152]{0:T(1024)} %get-tuple-element.202) | copy-start | bytes 13828
  (31 other events, 71.5 us)
Sparse Core Ops, SparseCore 0:
  13.5 79.1 all-gather.13
  128.4 38.0 all-gather.11
  256.1 47.8 reduce-scatter.12
  306.2 55.0 all-gather.17
  363.4 36.0 all-gather.15
  401.7 55.0 all-gather.23
  459.0 36.0 all-gather.21
  497.4 55.0 all-gather.25
  554.9 53.5 all-gather.19
  611.1 46.4 reduce-scatter.16
  660.1 47.8 reduce-scatter.14
  716.0 37.4 all-gather.27
  755.9 48.9 all-gather.29
  858.3 47.9 reduce-scatter.18
  925.5 29.3 reduce-scatter.30
  959.4 158.5 reduce-scatter.28
  1122.0 103.9 reduce-scatter.26
  1230.4 66.0 reduce-scatter.24
  1300.6 86.5 reduce-scatter.22
  1391.7 146.5 reduce-scatter.20
